TPU v7x, 32 devices: a whole 2x2x4 slice. The times are simulated.
32 devices in a mesh: design: 8 (over z, x), feat: 4 (over y, core).
Axes of the slice: x: 2, y: 2, z: 4, core: 2. Of those that a mesh axis runs over, the one named last changes fastest.
Arguments:
- table: bfloat16 [32768, 1024], P('design', 'feat'), may hold values from -0.29882812 to 0.29882812
- proj_weight: float32 [1024, 128], P('feat'), may hold values from -0.1875 to 0.1875
- anchor_ids: int32 [4096], P('design'), may hold values from 0 to 32767, as said below
- positive_ids: int32 [4096], P('design'), may hold values from 0 to 32767, as said below
- neg_tiles: int32 [32, 16], P('design'), may hold values from 0 to 255, as said below
Outputs:
- losses: float32 [4096], P('design')
- table_grad: float32 [32768, 1024], P('design', 'feat')
- weight_grad: float32 [1024, 128], P('feat')
Inputs may be any that keep to these rules, and one draw needn't show every extreme that they name: `anchor_ids`: entry i lies in the rows held by design index i // 512, that is from that index times 4096 on, 4096 rows. `positive_ids`: entry i lies in the rows held by design index i // 512, that is from that index times 4096 on, 4096 rows. `neg_tiles`: tile t is held by design index t // 32. Among the 4 rows of blocks of one design index, at most 16 entries name tiles held by any one index, and exactly 16 for some index.
All inputs are finite; a program needn't handle non-finite values.
Results may differ from a plain program's by a relative error of at most 0.0004.
Values may be sent and summed in bfloat16 or wider, within the bound.
A program may use at most 192 MiB of HBM per device.

v0:
```python
import jax
import jax.numpy as jnp
from jax import lax
from jax.sharding import PartitionSpec as P

TILE = 128


SOFTMAX_TEMP = 0.07
EPSILON = 1e-06


def unit_rows(values):
    return values / jnp.sqrt(jnp.sum(values * values, axis=-1, keepdims=True) + EPSILON)


def block_losses(anchor_z, positive_z, negative_z):
    anchor_unit_vector = unit_rows(anchor_z)
    positive_unit_vector = unit_rows(positive_z)
    negative_unit_vector = unit_rows(negative_z)
    positive_similarity = jnp.sum(anchor_unit_vector * positive_unit_vector, axis=-1) / SOFTMAX_TEMP
    negative_similarity = (
        jnp.einsum(
            "kjc,koc->kjo",
            anchor_unit_vector,
            negative_unit_vector,
            precision=lax.Precision.HIGHEST,
        )
        / SOFTMAX_TEMP
    )
    total = jnp.exp(positive_similarity) + jnp.sum(jnp.exp(negative_similarity), axis=-1)
    return jnp.log(total) - positive_similarity


def full_dot(left, right):
    return jnp.dot(left, right, precision=lax.Precision.HIGHEST, preferred_element_type=jnp.float32)


def shards(table, proj_weight, anchor_ids, positive_ids, neg_tiles):
    n_design = lax.axis_size("design")
    my_index = lax.axis_index("design")
    shard_rows, width = table.shape
    code_width = proj_weight.shape[1]
    tiles_dev = shard_rows // TILE
    blocks, negs = neg_tiles.shape
    wanted = blocks * negs
    capacity = 2 * wanted // n_design
    slot_count = n_design * capacity
    anchor_local = anchor_ids - my_index * shard_rows
    positive_local = positive_ids - my_index * shard_rows
    flat_tiles = neg_tiles.reshape(wanted)
    owner_dev = flat_tiles // tiles_dev
    local_tile = flat_tiles - owner_dev * tiles_dev
    request_order = jnp.arange(wanted, dtype=jnp.int32)
    earlier = (owner_dev[:, None] == owner_dev[None, :]) & (
        request_order[:, None] < request_order[None, :]
    )
    slot_rank = jnp.sum(earlier.astype(jnp.int32), axis=0)
    slot_position = owner_dev * capacity + slot_rank
    request = jnp.zeros((slot_count,), jnp.int32).at[slot_position].set(local_tile)
    asked = lax.all_to_all(
        request.reshape(n_design, capacity), "design", split_axis=0, concat_axis=0, tiled=True
    ).reshape(slot_count)
    own_embed = table.astype(jnp.float32)
    anchor_part = full_dot(own_embed[anchor_local], proj_weight)
    positive_part = full_dot(own_embed[positive_local], proj_weight)
    anchor_z, positive_z = lax.psum((anchor_part, positive_part), "feat")
    outgoing = table.reshape(tiles_dev, TILE, width)[asked].reshape(n_design, capacity, TILE, width)
    arrived = lax.all_to_all(outgoing, "design", split_axis=0, concat_axis=0, tiled=True).reshape(
        slot_count, TILE, width
    )
    negative_embed = arrived[slot_position].reshape(wanted * TILE, width).astype(jnp.float32)
    negative_z = lax.psum(full_dot(negative_embed, proj_weight), "feat")
    losses, pullback = jax.vjp(
        block_losses,
        anchor_z.reshape(blocks, TILE, code_width),
        positive_z.reshape(blocks, TILE, code_width),
        negative_z.reshape(blocks, negs * TILE, code_width),
    )
    anchor_grad, positive_grad, negative_grad = pullback(jnp.ones_like(losses))
    code_grad = jnp.zeros((shard_rows, code_width), jnp.float32)
    code_grad = code_grad.at[anchor_local].add(anchor_grad.reshape(-1, code_width))
    code_grad = code_grad.at[positive_local].add(positive_grad.reshape(-1, code_width))
    negative_tiles_grad = negative_grad.reshape(wanted, TILE, code_width)
    negative_rows_grad = negative_tiles_grad.reshape(wanted * TILE, code_width)
    embed_grad = full_dot(negative_rows_grad, proj_weight.T).reshape(wanted, TILE, width)
    weight_part = full_dot(own_embed.T, code_grad) + full_dot(negative_embed.T, negative_rows_grad)
    send_back = jnp.zeros((slot_count, TILE, width), jnp.float32).at[slot_position].set(embed_grad)
    returned = lax.all_to_all(
        send_back.reshape(n_design, capacity, TILE, width).astype(jnp.bfloat16),
        "design",
        split_axis=0,
        concat_axis=0,
        tiled=True,
    ).astype(jnp.float32)
    table_grad = full_dot(code_grad, proj_weight.T).reshape(tiles_dev, TILE, width)
    table_grad = (
        table_grad.at[asked]
        .add(returned.reshape(slot_count, TILE, width))
        .reshape(shard_rows, width)
    )
    weight_grad = lax.psum(weight_part, "design")
    return (losses.reshape(blocks * TILE), table_grad, weight_grad)


def solution(mesh):
    in_specs = (P("design", "feat"), P("feat", None), P("design"), P("design"), P("design", None))
    out_specs = (P("design"), P("design", "feat"), P("feat", None))
    return jax.shard_map(shards, mesh=mesh, in_specs=in_specs, out_specs=out_specs, check_vma=False)
```

profile of v0, /device:TPU:24, one launch (start us, length us, event | category | flops | bytes accessed | tf_op | source)
XLA Modules:
  0.0 664.3 jit_solution(4649962688690059816)
XLA Ops:
  7.2 0.0 copy-start
  7.2 0.9 reshape.332
  8.1 0.8 reshape.331
  8.9 0.1 convert_reduce_fusion
  9.0 0.8 scatter_custom_fusion
  9.8 0.1 all_to_all.12
  9.8 9.1 %all_to_all.19 = s32[8,1,16]{2,1,0:T(1,128)S(1)} all-to-all(s32[8,1,16]{2,1,0:T(1,128)S(1)} %bitcast.88), channel_id=1, replica_groups=mesh['design'=8,'feat'=4] {'design'}, dimensions={0} | all-to-all | bytes 1024 | tf_op jit(solution)/shard_map/all_to_all | solution.py:61
  18.9 0.5 broadcast.326
  19.4 0.7 reduce.8
  20.1 0.1 reshape.333
  20.2 6.3 gather_fusion.2
  26.5 8.4 %all-to-all-start.1 = ((bf16[8,16,128,256]{3,2,1,0:T(8,128)(2,1)}), bf16[8,16,128,256]{3,2,1,0:T(8,128)(2,1)}, u32[]{:S(2)}, u32[]{:S(2)}) async-start(bf16[8,16,128,256]{3,2,1,0:T(8,128)(2,1)} %bitcast.82), calls=%async_computation.1 | async-start | bytes 16777216 | tf_op jit(solution)/shard_map/all_to_all | solution.py:69
  34.9 2.0 gather_fusion
  36.9 2.0 gather_fusion.1
  38.9 1.1 fusion.32
  39.9 1.1 fusion.33
  41.0 174.3 %all-to-all-done.1 = bf16[8,16,128,256]{3,2,1,0:T(8,128)(2,1)} async-done(((bf16[8,16,128,256]{3,2,1,0:T(8,128)(2,1)}), bf16[8,16,128,256]{3,2,1,0:T(8,128)(2,1)}, u32[]{:S(2)}, u32[]{:S(2)}) %all-to-all-start.1) | async-done | bytes 8388640 | tf_op jit(solution)/shard_map/all_to_all | solution.py:69
  215.3 6.2 gather_fusion.3
  221.5 7.5 %fusion.34 = f32[8192,128]{1,0:T(8,128)} fusion(bf16[8192,256]{1,0:T(8,128)(2,1)} %bitcast.74, f32[256,128]{1,0:T(8,128)S(1)} %copy-done.7), kind=kOutput, calls=%fused_computation.98 | convolution fusion | flops 3221225472 | bytes 8519680 | tf_op jit(solution)/shard_map/dot_general | solution.py:36
  229.1 0.0 all-reduce.6.cloned.1.call-update
  229.1 94.3 %all-reduce.6.cloned.1.call-done = (f32[8192,128]{1,0:T(8,128)}, f32[512,128]{1,0:T(8,128)}, f32[512,128]{1,0:T(8,128)}) async-done(((f32[8192,128]{1,0:T(8,128)}, f32[512,128]{1,0:T(8,128)}, f32[512,128]{1,0:T(8,128)}), (f32[8192,128]{1,0:T(8,128)}, f32[512,128]{1,0:T(8,128)}, f32[512,128]{1,0:T(8,128)})) %all-reduce.6.cloned.1.call-update) | async-done | bytes 4718608 | tf_op jit(solution)/shard_map/psum | solution.py:73
  323.4 1.2 multiply_reduce_fusion.6
  324.6 1.1 multiply_reduce_fusion.5
  325.7 3.3 multiply_reduce_fusion.1
  329.2 0.3 multiply_reduce_fusion.4
  329.5 7.1 %fusion = (f32[4,128]{1,0:T(4,128)S(1)}, f32[4,128,2048]{2,1,0:T(8,128)S(1)}) fusion(f32[4,2048,128]{2,1,0:T(8,128)} %bitcast.78, f32[4,2048]{1,0:T(4,128)S(1)} %sqrt.60, f32[4,128,128]{2,1,0:T(8,128)S(1)} %bitcast.83, f32[4,128]{1,0:T(4,128)S(1)} %get-tuple-element.28), kind=kOutput, calls=%fused_computation.15 | convolution fusion | flops 1613823488 | bytes 8687616 | tf_op jit(solution)/shard_map/jvp(kjc,koc->kjo)/dot_general | solution.py:23
  336.7 9.5 %multiply_reduce_fusion = (f32[4,2048]{1,0:T(4,128)S(1)}, f32[4,2048,128]{2,1,0:T(8,128)S(1)}) fusion(f32[4,2048,128]{2,1,0:T(8,128)S(1)} %bitcast.80, f32[4,2048]{1,0:T(4,128)S(1)} %multiply_divide_fusion, f32[4,128,128]{2,1,0:T(8,128)S(1)} %bitcast.84, f32[4,128]{1,0:T(4,128)S(1)} %get-tuple-element.28, f32[4,128,2048]{2,1,0:T(8,128)S(1)} %get-tuple-element.30, ...), kind=kOutput, calls=%fused_computation.11 | convolution fusion | flops 1616961536 | bytes 12914688 | tf_op jit(solution)/shard_map/transpose(jvp(kjc,koc->kjo))/dot_general | solution.py:23
  346.2 2.5 add_add_fusion
  348.7 1.9 copy-done.2
  350.7 8.9 %fusion.15 = f32[64,128,256]{2,1,0:T(8,128)} fusion(f32[64,128,128]{2,1,0:T(8,128)S(1)} %bitcast.76, f32[256,128]{1,0:T(8,128)S(1)} %copy-done.7), kind=kOutput, calls=%fused_computation.40 | convolution fusion | flops 3221225472 | bytes 12713984 | tf_op jit(solution)/shard_map/dot_general | solution.py:36
  359.5 7.8 %broadcast_in_dim.61 = f32[128,128,256]{2,1,0:T(8,128)} broadcast(f32[]{:T(128)} %constant.21.clone.1), dimensions={} | broadcast | bytes 16777220 | tf_op jit(solution)/shard_map/broadcast_in_dim | solution.py:88
  367.4 16.2 %scatter_fusion = f32[128,128,256]{2,1,0:T(8,128)} fusion(f32[128,128,256]{2,1,0:T(8,128)} %broadcast_in_dim.61, s32[64]{0:T(128)S(1)} %fusion.24, f32[64,128,256]{2,1,0:T(8,128)} %fusion.15), kind=kCustom, calls=%fused_computation.7 | custom fusion | bytes 25166080 | tf_op jit(solution)/shard_map/scatter | solution.py:88
  383.5 9.0 %convert_element_type.13 = bf16[128,128,256]{2,1,0:T(8,128)(2,1)} convert(f32[128,128,256]{2,1,0:T(8,128)} %scatter_fusion) | non-fusion elementwise | flops 4194304 | bytes 25165824 | tf_op jit(solution)/shard_map/convert_element_type | solution.py:90
  392.5 6.0 all-to-all-start.2
  398.5 0.6 add_multiply_fusion
  399.1 0.4 multiply_reduce_fusion.2
  399.5 8.1 %multiply_reduce_fusion.3 = (f32[4,128]{1,0:T(4,128)S(1)}, f32[4,128,128]{2,1,0:T(8,128)S(1)}) fusion(f32[4,128,128]{2,1,0:T(8,128)S(1)} %bitcast.85, f32[4,128]{1,0:T(4,128)S(1)} %multiply_divide_fusion.2, f32[4,128,128]{2,1,0:T(8,128)S(1)} %bitcast.86, f32[4,128]{1,0:T(4,128)S(1)} %get-tuple-element.24, f32[4,128]{1,0:T(4,128)S(1)} %get-tuple-element.21, ...), kind=kOutput, calls=%fused_computation.35 | convolution fusion | flops 1615199744 | bytes 9218048 | tf_op jit(solution)/shard_map/transpose(jvp(kjc,koc->kjo))/dot_general | solution.py:23
  407.6 0.2 add_add_fusion.2
  407.8 3.6 scatter_custom_fusion.1
  411.4 6.5 scatter_custom_fusion.2
  417.9 3.5 convolution_bitcast_fusion
  421.5 6.4 convolution_add_fusion
  427.9 0.0 all-reduce.4.cloned.1.call-update
  427.9 7.0 %fusion.35 = f32[4096,256]{1,0:T(8,128)} fusion(f32[4096,128]{1,0:T(8,128)} %scatter_custom_fusion.2, f32[256,128]{1,0:T(8,128)S(1)} %copy-done.7), kind=kOutput, calls=%fused_computation.99 | convolution fusion | flops 1610612736 | bytes 6422528 | tf_op jit(solution)/shard_map/dot_general | solution.py:36
  435.0 168.0 %all-reduce.4.cloned.1.call-done = f32[256,128]{0,1:T(8,128)} async-done(((f32[256,128]{0,1:T(8,128)}), f32[256,128]{0,1:T(8,128)}) %all-reduce.4.cloned.1.call-update) | async-done | bytes 131088 | tf_op jit(solution)/shard_map/psum | solution.py:102
  602.9 1.7 copy.18
  604.6 11.5 %bitcast_convert_fusion = f32[128,128,256]{2,1,0:T(8,128)} fusion(bf16[8,16,128,256]{3,2,1,0:T(8,128)(2,1)} %all-to-all-done.2), kind=kLoop, calls=%fused_computation.9 | loop fusion | flops 4194304 | bytes 25165824 | tf_op jit(solution)/shard_map/reshape | solution.py:99
  616.0 41.0 %scatter_fusion.1 = f32[32,128,256]{2,1,0:T(8,128)} fusion(f32[32,128,256]{2,1,0:T(8,128)} %bitcast.72, s32[128]{0:T(128)S(1)} %fusion.25, f32[128,128,256]{2,1,0:T(8,128)} %bitcast_convert_fusion), kind=kCustom, calls=%fused_computation.8 | custom fusion | flops 4194304 | bytes 50332160 | tf_op jit(solution)/shard_map/scatter-add | solution.py:99
  (40 shorter events, 0.2 us)
Async XLA Ops:
  7.2 13.0 %copy-start = (bf16[4096,256]{1,0:T(8,128)(2,1)S(1)}, bf16[4096,256]{1,0:T(8,128)(2,1)}, u32[]{:S(2)}) copy-start(bf16[4096,256]{1,0:T(8,128)(2,1)} %param.5) | copy-start | bytes 6291460
  26.5 8.4 %copy-start.8 = (s32[512]{0:T(512)S(1)}, s32[512]{0:T(512)}, u32[]{:S(2)}) copy-start(s32[512]{0:T(512)} %param.8) | copy-start | bytes 6148
  26.5 8.4 %copy-start.9 = (s32[512]{0:T(512)S(1)}, s32[512]{0:T(512)}, u32[]{:S(2)}) copy-start(s32[512]{0:T(512)} %param.7) | copy-start | bytes 6148
  26.5 188.9 %all-to-all-start.1 = ((bf16[8,16,128,256]{3,2,1,0:T(8,128)(2,1)}), bf16[8,16,128,256]{3,2,1,0:T(8,128)(2,1)}, u32[]{:S(2)}, u32[]{:S(2)}) async-start(bf16[8,16,128,256]{3,2,1,0:T(8,128)(2,1)} %bitcast.82), calls=%async_computation.1 | async-start | bytes 16777216 | tf_op jit(solution)/shard_map/all_to_all | solution.py:69
  34.9 4.0 copy-start.7
  34.9 288.5 %all-reduce.6.cloned.1.call-start = ((), (), s32[]{:S(2)}) async-start(), calls=%async_computation.4 | async-start | bytes 9437184 | tf_op jit(solution)/shard_map/psum | solution.py:73
  323.4 5.7 copy-start.4
  323.4 5.8 copy-start.5
  329.5 7.2 %copy-start.3 = (f32[8192,128]{1,0:T(8,128)S(1)}, f32[8192,128]{1,0:T(8,128)}, u32[]{:S(2)}) copy-start(f32[8192,128]{1,0:T(8,128)} %get-tuple-element.12) | copy-start | bytes 12582916
  336.6 9.6 %copy-start.6 = (f32[4,128,2048]{2,1,0:T(8,128)}, f32[4,128,2048]{2,1,0:T(8,128)S(1)}, u32[]{:S(2)}) copy-start(f32[4,128,2048]{2,1,0:T(8,128)S(1)} %get-tuple-element.30) | copy-start | bytes 12582916
  348.7 1.9 copy-start.2
  392.5 212.1 %all-to-all-start.2 = ((bf16[8,16,128,256]{3,2,1,0:T(8,128)(2,1)}), bf16[8,16,128,256]{3,2,1,0:T(8,128)(2,1)}, u32[]{:S(2)}, u32[]{:S(2)}) async-start(bf16[8,16,128,256]{3,2,1,0:T(8,128)(2,1)} %bitcast.81), calls=%async_computation.2 | async-start | bytes 16777216 | tf_op jit(solution)/shard_map/all_to_all | solution.py:89
  398.5 204.4 %all-reduce.4.cloned.1.call-start = ((), (), s32[]{:S(2)}) async-start(), calls=%async_computation.3 | async-start | bytes 262144 | tf_op jit(solution)/shard_map/psum | solution.py:102
  417.9 3.6 copy-start.1
Sparse Core Ops, SparseCore 0:
  229.2 94.1 all-reduce.5
  428.1 174.8 all-reduce.3
where the time goes:
time: 674 us; the launch traced here: 664 us
  waiting for transfers between devices  437 us (65%)
  other arithmetic  82 us (12%)
  matrix products  60.3 us (9%)
  local copies, waits for them, and re-layouts  47.2 us (7%)
  between operations  14.8 us (2%)
  starting transfers between devices  14.4 us (2%)
  blocking collectives  9.05 us (1%)
    all_to_all x1, waiting for transfers between devices, shards(): lax.all_to_all(outgoing, 'design', split_axis=0, concat_axis=0, tiled=True)  174 us
    psum x1, waiting for transfers between devices, shards(): weight_grad = lax.psum(weight_part, 'design')  168 us
    psum x1, waiting for transfers between devices, shards(): negative_z = lax.psum(full_dot(negative_embed, proj_weight), 'feat')  94.3 us
    scatter-add x1, other arithmetic, shards(): table_grad = table_grad.at[asked].add(returned.reshape(slot_count, TILE,...  41 us
    dot_general x7, matrix products, full_dot(): jnp.dot(left, right, precision=lax.Precision.HIGHEST, preferred_element_t...  35.6 us
    dot_general x3, matrix products, block_losses(): jnp.einsum('kjc,koc->kjo', anchor_unit_vector, negative_unit_vector, prec...  24.7 us
    scatter x1, local copies, waits for them, and re-layouts, shards(): jnp.zeros((slot_count, TILE, width), jnp.float32).at[slot_position]  16.2 us
  transfers between devices with their start and end apart: 4, of which 3 were waited for; matrix products, arithmetic and copies ran while one was open for 7% of the time, Pallas kernels for 0%

commit v1 on v0

v1 whole, which is shorter than its diff:
```python
import functools

import jax
import jax.numpy as jnp
from jax import lax
from jax.experimental import pallas as pl
from jax.experimental.pallas import tpu as pltpu
from jax.sharding import PartitionSpec as P

TILE = 128
SCALE = 1.0 / 0.07
EPSILON = 1e-06
F32 = jnp.float32
BF16 = jnp.bfloat16
VM = pl.BlockSpec(memory_space=pltpu.VMEM)
SM = pl.BlockSpec(memory_space=pltpu.SMEM)
BIG = pltpu.CompilerParams(vmem_limit_bytes=56 * 1024 * 1024)


def split(v):
    hi = v.astype(BF16)
    return hi, (v - hi.astype(F32)).astype(BF16)


def dot(a, b, ca=1, cb=0):
    return lax.dot_general(a, b, (((ca,), (cb,)), ((), ())), preferred_element_type=F32)


def radius(z):
    return jnp.sqrt(jnp.sum(z * z, axis=-1, keepdims=True) + EPSILON)


def project_kernel(feats, own, aid_ref, pid_ref, table_ref, w_ref, out_ref):
    chunk = table_ref.shape[0] // feats
    stride = chunk + 2 * own
    hi, lo = split(w_ref[...])
    w2 = jnp.concatenate([hi, lo], axis=1)
    width = w_ref.shape[1]
    for c in range(feats):
        both = dot(table_ref[c * chunk : (c + 1) * chunk, :], w2)
        out_ref[c * stride : c * stride + chunk, :] = both[:, :width] + both[:, width:]
    for ids, at in ((aid_ref, chunk), (pid_ref, chunk + own)):
        for c in range(feats):

            def take(i, _):
                for k in range(8):
                    j = i * 8 + k
                    row = ids[c * own + j]
                    source = row + (row // chunk) * (2 * own)
                    out_ref[pl.ds(c * stride + at + j, 1), :] = out_ref[pl.ds(source, 1), :]
                return 0

            lax.fori_loop(0, own // 8, take, 0)


def list_pairs(tiles_ref, first_ref, pairs, mine, negs):
    first = first_ref[0]

    def scan(i, count):
        for k in range(8):
            t = tiles_ref[i * 8 + k] - first
            pairs[count] = ((i * 8 + k) // negs) * mine + t
            count = count + ((t >= 0) & (t < mine)).astype(jnp.int32)
        return count

    return lax.fori_loop(0, tiles_ref.shape[0] // 8, scan, 0)


def similar_t(n_ref, a_hi, a_lo, row):
    nh = n_ref[0, pl.ds(row, TILE), :]
    nl = n_ref[1, pl.ds(row, TILE), :]
    left = jnp.concatenate([nh, nl, nh], axis=1)
    right = jnp.concatenate([a_hi, a_hi, a_lo], axis=1)
    return jnp.exp(dot(left, right, 1, 1) * SCALE)


def forward_kernel(negs, tiles_ref, first_ref, a_ref, z_ref, u_ref, n_ref, pairs):
    mine = z_ref.shape[0] // TILE
    z = z_ref[...]
    unit = z / radius(z)
    n_ref[0], n_ref[1] = split(unit)
    u_ref[...] = jnp.zeros_like(u_ref)
    count = list_pairs(tiles_ref, first_ref, pairs, mine, negs)

    def pair(i, _):
        code = pairs[i]
        b = code // mine
        row = pl.multiple_of((code - b * mine) * TILE, TILE)
        a_hi, a_lo = split(a_ref[b])
        e = similar_t(n_ref, a_hi, a_lo, row)
        u_ref[b, TILE : TILE + 1, :] += jnp.sum(e, axis=0, keepdims=True)
        eh, el = split(e.T)
        nh = n_ref[0, pl.ds(row, TILE), :]
        nl = n_ref[1, pl.ds(row, TILE), :]
        u_ref[b, :TILE, :] += dot(
            jnp.concatenate([eh, el, eh], axis=1), jnp.concatenate([nh, nh, nl], axis=0)
        )
        return 0

    lax.fori_loop(0, count, pair, 0)

    def project(b, _):
        a = a_ref[b]
        u = u_ref[b, :TILE, :]
        u_ref[b, :TILE, :] = u - jnp.sum(u * a, axis=-1, keepdims=True) * a
        return 0

    lax.fori_loop(0, a_ref.shape[0], project, 0)


def backward_kernel(negs, tiles_ref, first_ref, a_ref, z_ref, inv_ref, out_ref, n_ref, acc, pairs):
    mine = z_ref.shape[0] // TILE
    z = z_ref[...]
    r = radius(z)
    unit = z / r
    n_ref[0], n_ref[1] = split(unit)
    acc[...] = jnp.zeros_like(acc)
    count = list_pairs(tiles_ref, first_ref, pairs, mine, negs)

    def pair(i, _):
        code = pairs[i]
        b = code // mine
        row = pl.multiple_of((code - b * mine) * TILE, TILE)
        a_hi, a_lo = split(a_ref[b])
        p = similar_t(n_ref, a_hi, a_lo, row) * inv_ref[pl.ds(b, 1), :]
        ph, pll = split(p)
        acc[pl.ds(row, TILE), :] += dot(
            jnp.concatenate([ph, pll, ph], axis=1), jnp.concatenate([a_hi, a_hi, a_lo], axis=0)
        )
        return 0

    lax.fori_loop(0, count, pair, 0)
    g = acc[...]
    g = (g - jnp.sum(g * unit, axis=-1, keepdims=True) * unit) * (SCALE / r)
    out_ref[...] = g.astype(BF16)


def final_kernel(feats, own, aid_ref, pid_ref, table_ref, w_ref, dn_ref, g_ref, tg_ref, wg_ref, cg):
    rows = table_ref.shape[0]
    width = w_ref.shape[1]
    cg[...] = dn_ref[...].astype(F32)
    for ids, at in ((aid_ref, 0), (pid_ref, own)):
        for c in range(feats):

            def put(i, _):
                for k in range(8):
                    j = i * 8 + k
                    row = ids[c * own + j]
                    cg[pl.ds(row, 1), :] += g_ref[pl.ds(c * 2 * own + at + j, 1), :]
                return 0

            lax.fori_loop(0, own // 8, put, 0)
    wh, wl = split(w_ref[...])
    w3 = jnp.concatenate([wh, wh, wl], axis=1)
    chunk = rows // feats
    total = jnp.zeros((table_ref.shape[1], 2 * width), F32)
    for c in range(feats):
        ch, cl = split(cg[c * chunk : (c + 1) * chunk, :])
        tg_ref[c * chunk : (c + 1) * chunk, :] = dot(jnp.concatenate([ch, cl, ch], axis=1), w3, 1, 1)
        total += dot(
            table_ref[c * chunk : (c + 1) * chunk, :], jnp.concatenate([ch, cl], axis=1), 0, 0
        )
    wg_ref[...] = total[:, :width] + total[:, width:]


def call(kernel, out, args, smem, scratch=()):
    return pl.pallas_call(
        kernel,
        out_shape=out,
        in_specs=[SM if i < smem else VM for i in range(len(args))],
        out_specs=jax.tree.map(lambda _: VM, out),
        scratch_shapes=list(scratch),
        compiler_params=BIG,
    )(*args)


def shards(table, proj_weight, anchor_ids, positive_ids, neg_tiles):
    feats = lax.axis_size("feat")
    design = lax.axis_index("design")
    feat = lax.axis_index("feat")
    both = ("design", "feat")
    rows, depth = table.shape
    width = proj_weight.shape[1]
    blocks, negs = neg_tiles.shape
    own = blocks * TILE // feats
    chunk = rows // feats
    mine = chunk // TILE
    stride = chunk + 2 * own
    shape = jax.ShapeDtypeStruct
    aid = anchor_ids - design * rows
    pid = positive_ids - design * rows
    tiles = lax.all_gather(neg_tiles, "design", tiled=True).reshape(-1)
    first = ((design * feats + feat) * mine).astype(jnp.int32).reshape(1)

    part = call(
        functools.partial(project_kernel, feats, own),
        shape((feats * stride, width), F32),
        (aid, pid, table, proj_weight),
        2,
    )
    mine_z = lax.psum_scatter(part, "feat", scatter_dimension=0, tiled=True)
    z, za, zp = mine_z[:chunk], mine_z[chunk : chunk + own], mine_z[chunk + own :]
    ra, rp = radius(za), radius(zp)
    a, p = za / ra, zp / rp
    every = lax.all_gather(a, both, tiled=True).reshape(-1, TILE, width)
    count = every.shape[0]
    pair_cap = tiles.shape[0] + 8
    u = call(
        functools.partial(forward_kernel, negs),
        shape((count, TILE + 8, width), F32),
        (tiles, first, every, z),
        2,
        (pltpu.VMEM((2, chunk, width), BF16), pltpu.SMEM((pair_cap,), jnp.int32)),
    )
    u = lax.psum_scatter(u, both, scatter_dimension=0, tiled=True)
    s = u[:, TILE, :].reshape(own)
    u = u[:, :TILE, :].reshape(own, width)
    dots = jnp.sum(a * p, axis=-1)
    pos = dots * SCALE
    total = jnp.exp(pos) + s
    losses = jnp.log(total) - pos
    inv = (1.0 / total).reshape(own // TILE, TILE)
    rest = (s / total)[:, None]
    ga = (u / total[:, None] - rest * (p - dots[:, None] * a)) * (SCALE / ra)
    gp = rest * (dots[:, None] * p - a) * (SCALE / rp)
    grads = lax.all_gather(jnp.concatenate([ga, gp], axis=0), "feat", tiled=True)
    losses = lax.all_gather(losses, "feat", tiled=True)
    invs = lax.all_gather(inv, both, tiled=True)
    dn = call(
        functools.partial(backward_kernel, negs),
        shape((chunk, width), BF16),
        (tiles, first, every, z, invs),
        2,
        (
            pltpu.VMEM((2, chunk, width), BF16),
            pltpu.VMEM((chunk, width), F32),
            pltpu.SMEM((pair_cap,), jnp.int32),
        ),
    )
    dn = lax.all_gather(dn, "feat", tiled=True)
    table_grad, weight_part = call(
        functools.partial(final_kernel, feats, own),
        (shape((rows, depth), F32), shape((depth, width), F32)),
        (aid, pid, table, proj_weight, dn, grads),
        2,
        (pltpu.VMEM((rows, width), F32),),
    )
    weight_grad = lax.psum(weight_part, "design")
    return losses, table_grad, weight_grad


def solution(mesh):
    in_specs = (P("design", "feat"), P("feat", None), P("design"), P("design"), P("design", None))
    out_specs = (P("design"), P("design", "feat"), P("feat", None))
    return jax.shard_map(shards, mesh=mesh, in_specs=in_specs, out_specs=out_specs, check_vma=False)
```

time: 674 us -> 433 us (0.64); the launches traced: 664 us -> 434 us
  waiting for transfers between devices: 437 us -> 289 us
  other arithmetic: 82 us -> 5.65 us
  blocking collectives: 9.05 us -> 70 us
  matrix products: 60.3 us -> 0 us
  Pallas kernels: 0 us -> 50.7 us
  local copies, waits for them, and re-layouts: 47.2 us -> 4.71 us
  starting transfers between devices: 14.4 us -> 0.21 us
    all_to_all x2 -> x0, waiting for transfers between devices: 174 us -> none  [the longest x1 174 us: shards(): lax.all_to_all(outgoing, 'design', split_axis=0, concat_axis=0, tiled=True)]
    unnamed x2 -> x6, waiting for transfers between devices: 0.03 us -> 141 us
    psum x1, waiting for transfers between devices: 168 us -> 64.6 us  [shards(): weight_grad = lax.psum(weight_part, 'design')]
    psum x1 -> x0, waiting for transfers between devices: 94.3 us -> none  [shards(): negative_z = lax.psum(full_dot(negative_embed, proj_weight), 'feat')]
    all_gather x0 -> x4, blocking collectives: none -> 70 us  [the longest x1 32.8 us: shards(): invs = lax.all_gather(inv, both, tiled=True)]
    dot_general x10 -> x0, matrix products: 60.3 us -> none  [the longest x7 35.6 us: full_dot(): jnp.dot(left, right, precision=lax.Precision.HIGHEST, preferred_element_t...]
    scatter-add x3 -> x0, other arithmetic: 51.1 us -> none  [the longest x1 41 us: shards(): table_grad = table_grad.at[asked].add(returned.reshape(slot_count, TILE,...]
    pallas_call x0 -> x4, Pallas kernels: none -> 50.7 us  [call(): pl.pallas_call(kernel, out_shape=out, in_specs=[SM if i < smem else VM fo...]
  transfers between devices with their start and end apart: 4 -> 5, of which waited for: 3 -> 5; matrix products, arithmetic and copies ran while one was open for 7% -> 1% of each run, Pallas kernels for 0% -> 0%
where the time goes in v1:
time: 433 us; the launch traced here: 434 us
  waiting for transfers between devices  289 us (67%)
  blocking collectives  70 us (16%)
  Pallas kernels  50.7 us (12%)
  between operations  13.9 us (3%)
  other arithmetic  5.65 us (1%)
  local copies, waits for them, and re-layouts  4.71 us (1%)
    unnamed x6, waiting for transfers between devices  141 us
    psum x1, waiting for transfers between devices, shards(): weight_grad = lax.psum(weight_part, 'design')  64.6 us
    pallas_call x4, Pallas kernels, call(): pl.pallas_call(kernel, out_shape=out, in_specs=[SM if i < smem else VM fo...  50.7 us
    reduce_scatter x1, waiting for transfers between devices, shards(): mine_z = lax.psum_scatter(part, 'feat', scatter_dimension=0, tiled=True)  35.6 us
    all_gather x1, blocking collectives, shards(): invs = lax.all_gather(inv, both, tiled=True)  32.8 us
    all_gather x1, waiting for transfers between devices, shards(): every = lax.all_gather(a, both, tiled=True).reshape(-1, TILE, width)  30.8 us
    all_gather x1, blocking collectives, shards(): tiles = lax.all_gather(neg_tiles, 'design', tiled=True).reshape(-1)  22.5 us
    all_gather x1, waiting for transfers between devices, shards(): dn = lax.all_gather(dn, 'feat', tiled=True)  16.4 us
  transfers between devices with their start and end apart: 5, of which 5 were waited for; matrix products, arithmetic and copies ran while one was open for 1% of the time, Pallas kernels for 0%

profile of v1, /device:TPU:24, one launch (start us, length us, event | category | flops | bytes accessed | tf_op | source)
XLA Modules:
  0.0 433.8 jit_solution(1581223911853052189)
XLA Ops:
  7.2 0.0 reduce-scatter.2.cloned.1.call-start
  7.2 1.3 broadcast_subtract_fusion
  8.5 10.1 %shard_map.76 = f32[5120,128]{1,0:T(8,128)} custom-call(s32[512]{0:T(512)} %get-tuple-element.22.aid_ref, s32[512]{0:T(512)} %get-tuple-element.21.pid_ref, bf16[4096,256]{1,0:T(8,128)(2,1)} %table_ref.3, f32[256,128]{1,0:T(8,128)} %w_ref.3), custom_call_target="tpu_custom_call" | custom-call | tf_op jit(solution)/shard_map/pallas_call | solution.py:167
  18.6 0.0 copy-start.1
  18.6 0.0 reduce-scatter.2.cloned.1.call-update
  18.7 0.0 all-gather.6.cloned.1.call-start
  18.7 35.6 %reduce-scatter.2.cloned.1.call-done = f32[1280,128]{1,0:T(8,128)} async-done(((f32[5120,128]{1,0:T(8,128)}), f32[1280,128]{1,0:T(8,128)}) %reduce-scatter.2.cloned.1.call-update) | async-done | bytes 655376 | tf_op jit(solution)/shard_map/reduce_scatter | solution.py:201
  54.3 1.0 multiply_reduce_fusion.1
  55.3 1.6 multiply_reduce_fusion
  56.9 0.0 all-gather.6.cloned.1.call-update
  57.0 0.0 all-reduce.6.cloned.1.call-start
  57.0 0.0 copy-done.1
  57.0 22.5 %all-gather = s32[8,4,16]{2,1,0:T(4,128)S(1)} all-gather(s32[1,4,16]{2,1,0:T(4,128)S(1)} %bitcast.38), channel_id=1, replica_groups=mesh['design'=8,'feat'=4] {'design'}, dimensions={0}, use_global_device_ids=true | all-gather | bytes 2304 | tf_op jit(solution)/shard_map/all_gather | solution.py:192
  79.5 0.7 reshape.86.tiles_ref
  80.2 1.9 slice.22.z_ref
  82.1 30.8 %all-gather.6.cloned.1.call-done = f32[4096,128]{1,0:T(8,128)} async-done(((f32[128,128]{1,0:T(8,128)}), f32[4096,128]{1,0:T(8,128)}) %all-gather.6.cloned.1.call-update) | async-done | bytes 2097168 | tf_op jit(solution)/shard_map/all_gather | solution.py:205
  112.9 18.1 %shard_map.77 = f32[32,136,128]{2,1,0:T(8,128)} custom-call(s32[512]{0:T(512)} %reshape.86.tiles_ref, s32[1]{0:T(128)} %bitcast.1.first_ref, f32[32,128,128]{2,1,0:T(8,128)} %bitcast.34, f32[1024,128]{1,0:T(8,128)} %slice.22.z_ref), custom_call_target="tpu_custom_call" | custom-call | tf_op jit(solution)/shard_map/pallas_call | solution.py:167
  130.9 0.0 copy-start
  130.9 0.0 all-reduce.6.cloned.1.call-update
  130.9 0.0 all-gather.8.cloned.1.call-start
  131.0 141.3 %all-reduce.6.cloned.1.call-done = f32[32,136,128]{2,1,0:T(8,128)} async-done(((f32[32,136,128]{2,1,0:T(8,128)}), f32[32,136,128]{2,1,0:T(8,128)}) %all-reduce.6.cloned.1.call-update) | async-done | bytes 2228240
  272.3 0.7 bitcast_add_fusion.1
  273.0 32.8 %all-gather.2 = f32[32,1,128]{2,1,0:T(1,128)} all-gather(f32[1,1,128]{2,1,0:T(1,128)S(1)} %fusion.4), channel_id=1, replica_groups=mesh['design'=8,'feat'=4] {'design','feat'}, dimensions={0}, use_global_device_ids=true | all-gather | bytes 16896 | tf_op jit(solution)/shard_map/all_gather | solution.py:228
  305.8 13.4 %shard_map.78 = bf16[1024,128]{1,0:T(8,128)(2,1)} custom-call(s32[512]{0:T(512)} %reshape.86.tiles_ref, s32[1]{0:T(128)} %bitcast.1.first_ref, f32[32,128,128]{2,1,0:T(8,128)} %bitcast.35, f32[1024,128]{1,0:T(8,128)} %slice.22.z_ref, f32[32,128]{1,0:T(8,128)} %bitcast.36), custom_call_target="tpu_custom_call" | custom-call | tf_op jit(solution)/shard_map/pallas_call | solution.py:167
  319.2 0.0 all-gather.8.cloned.1.call-update
  319.2 0.0 all-reduce.4.cloned.1.call-start
  319.3 0.0 copy-done
  319.3 1.0 fusion.2
  320.4 9.6 %all_gather.23.g_ref = f32[1024,128]{1,0:T(8,128)} all-gather(f32[256,128]{1,0:T(8,128)S(1)} %pad_maximum_fusion), channel_id=1, replica_groups=mesh['design'=8,'feat'=4] {'feat'}, dimensions={0}, use_global_device_ids=true | all-gather | bytes 655360 | tf_op jit(solution)/shard_map/all_gather | solution.py:226
  329.9 16.4 %all-gather.8.cloned.1.call-done.dn_ref = bf16[4096,128]{1,0:T(8,128)(2,1)} async-done(((bf16[1024,128]{1,0:T(8,128)(2,1)}), bf16[4096,128]{1,0:T(8,128)(2,1)}) %all-gather.8.cloned.1.call-update) | async-done | bytes 1048592 | tf_op jit(solution)/shard_map/all_gather | solution.py:240
  346.4 9.1 %shard_map.79 = (f32[4096,256]{1,0:T(8,128)}, f32[256,128]{1,0:T(8,128)}) custom-call(s32[512]{0:T(512)} %get-tuple-element.22.aid_ref, s32[512]{0:T(512)} %get-tuple-element.21.pid_ref, bf16[4096,256]{1,0:T(8,128)(2,1)} %table_ref.3, f32[256,128]{1,0:T(8,128)} %w_ref.3, bf16[4096,128]{1,0:T(8,128)(2,1)} %all-gather.8.cloned.1.call-done.dn_ref, ...), custom_call_target="tpu_custom_call" | custom-call | tf_op jit(solution)/shard_map/pallas_call | solution.py:167
  355.4 0.0 all-reduce.4.cloned.1.call-update
  355.5 5.1 %all-gather.1 = f32[4,1,128]{2,1,0:T(1,128)S(1)} all-gather(f32[1,1,128]{2,1,0:T(1,128)S(1)} %get-tuple-element.16), channel_id=1, replica_groups=mesh['design'=8,'feat'=4] {'feat'}, dimensions={0}, use_global_device_ids=true | all-gather | bytes 2560 | tf_op jit(solution)/shard_map/all_gather | solution.py:227
  360.5 64.6 %all-reduce.4.cloned.1.call-done = f32[256,128]{1,0:T(8,128)} async-done(((f32[256,128]{1,0:T(8,128)}), f32[256,128]{1,0:T(8,128)}) %all-reduce.4.cloned.1.call-update) | async-done | bytes 131088 | tf_op jit(solution)/shard_map/psum | solution.py:248
  425.1 0.6 copy.12
  425.7 1.6 copy.13
  (5 shorter events, 0.0 us)
Async XLA Ops:
  7.2 47.1 %reduce-scatter.2.cloned.1.call-start = ((), (), s32[]{:S(2)}) async-start(), calls=%async_computation.1 | async-start | bytes 3276800 | tf_op jit(solution)/shard_map/reduce_scatter | solution.py:201
  18.6 38.4 %copy-start.1 = (s32[4,16]{1,0:T(4,128)S(1)}, s32[4,16]{1,0:T(4,128)}, u32[]{:S(2)}) copy-start(s32[4,16]{1,0:T(4,128)} %param.9) | copy-start | bytes 772
  18.7 94.2 %all-gather.6.cloned.1.call-start = ((), (), s32[]{:S(2)}) async-start(), calls=%async_computation.2 | async-start | bytes 2162688 | tf_op jit(solution)/shard_map/all_gather | solution.py:205
  57.0 215.3 %all-reduce.6.cloned.1.call-start = ((), (), s32[]{:S(2)}) async-start(), calls=%async_computation.5 | async-start | bytes 4456448
  130.9 188.4 %copy-start = (f32[128,128]{1,0:T(8,128)S(1)}, f32[128,128]{1,0:T(8,128)}, u32[]{:S(2)}) copy-start(f32[128,128]{1,0:T(8,128)} %get-tuple-element.12) | copy-start | bytes 196612
  130.9 215.4 %all-gather.8.cloned.1.call-start = ((), (), s32[]{:S(2)}) async-start(), calls=%async_computation.3 | async-start | bytes 1310720 | tf_op jit(solution)/shard_map/all_gather | solution.py:240
  319.2 105.9 %all-reduce.4.cloned.1.call-start = ((), (), s32[]{:S(2)}) async-start(), calls=%async_computation.4 | async-start | bytes 262144 | tf_op jit(solution)/shard_map/psum | solution.py:248
Sparse Core Ops, SparseCore 0:
  18.8 35.4 reduce-scatter.1
  57.7 55.0 all-gather.5
  131.1 141.1 all-reduce.5
  319.4 26.9 all-gather.7
  355.6 69.4 all-reduce.3
